TPU v7x, 256 devices: a whole 4x4x8 slice. The times are simulated.
256 devices in a mesh: lat: 64 (over x, y_hi, z), lon: 4 (over y_lo, core).
Axes of the slice: x: 4, y: 4 (y_hi: 2, y_lo: 2; y = y_hi * 2 + y_lo), z: 8, core: 2. Of those that a mesh axis runs over, the one named last changes fastest.
Arguments:
- tracer: float32 [32, 1536, 1152], P(None, 'lat', 'lon'), may hold values from -6 to 6
- wind_u: float32 [32, 1536, 1152], P(None, 'lat', 'lon'), may hold values from -2.5 to 2.5
- wind_v: float32 [32, 1536, 1152], P(None, 'lat', 'lon'), may hold values from -2.5 to 2.5
- ocean_temp: float32 [4, 2048, 3584], P(None, 'lat', 'lon'), may hold values from -6 to 6
- land_mask: int32 [2048, 3584], P('lat', 'lon'), may hold values 0 or 1
- remap_rows: int32 [2048, 3584], P('lat', 'lon'), may hold values from 0 to 1535, as said below
- remap_cols: int32 [2048, 3584], P('lat', 'lon'), may hold values from 0 to 1151, as said below
- polar_rows: int32 [192], replicated, may hold values from 0 to 1535, as said below
Outputs:
- tracer_out: float32 [32, 1536, 1152], P(None, 'lat', 'lon')
- ocean_out: float32 [4, 2048, 3584], P(None, 'lat', 'lon')
Inputs may be any that keep to these rules, and one draw needn't show every extreme that they name: `remap_rows`: for an ocean cell in row block b of 32 rows, an atmosphere row from b * 24 - 1 to (b + 1) * 24, within the grid. `remap_cols`: for an ocean cell in column block c of 896 columns, an atmosphere column from c * 288 - 1 to (c + 1) * 288, modulo 1152. `polar_rows`: distinct rows, each among the 192 rows nearest either pole.
All inputs are finite; a program needn't handle non-finite values. No bound on the sum of `land_mask` on one device may be relied on, other than what follows from the above.
Results may differ from a plain program's by a relative error of at most 0.0001.
Values sent between devices are 32-bit elements; how exact they have to be, the bound alone decides.
No kernel may reach another device: no remote copies, remote signals or barrier semaphores. Data moves between devices by JAX's collectives and lax.ppermute only.
A program may use at most 128 MiB of HBM per device.

v0:
```python
import math
import jax
import jax.numpy as jnp
from jax import lax
from jax.sharding import PartitionSpec as P

STEPS = 2
OSTEPS = 2
advect_coef = 0.2
diffuse_coef = 0.1
flux_coef = 0.25
ocean_diffuse = 0.15
vertical_mix = 0.2
highest = lax.Precision.HIGHEST


def padded_2(shard, sides, width, wrap):
    for axis, dim in sides:
        count, length = (lax.axis_size(axis), shard.shape[dim])
        up = [(i, (i + 1) % count) for i in range(count if wrap else count - 1)]
        down = [(j, i) for i, j in up]
        last = lax.slice_in_dim(shard, length - width, length, axis=dim)
        first = lax.slice_in_dim(shard, 0, width, axis=dim)
        before = lax.ppermute(last, axis, up)
        after = lax.ppermute(first, axis, down)
        shard = jnp.concatenate([before, shard, after], axis=dim)
    return shard


def damp_table(row_index, polar_rows, wave_numbers, lat_total, band_rows, lon_total):
    latitude_cos = jnp.sin(math.pi * (row_index.astype(jnp.float32) + 0.5) / lat_total)
    ratio = latitude_cos / math.sin(math.pi * band_rows / lat_total)
    wave_sine = jnp.sin(math.pi * wave_numbers / lon_total)
    safe_sine = jnp.where(wave_numbers > 0.5, wave_sine, 1.0)
    damping = jnp.where(
        wave_numbers[None, :] > 0.5, jnp.minimum(1.0, ratio[:, None] / safe_sine[None, :]), 1.0
    )
    listed = jnp.any(row_index[:, None] == polar_rows[None, :], axis=1)
    return jnp.where(listed[:, None], damping, 1.0)


def make_basis(lon_total):
    half_circle = lon_total // 2
    points = jnp.arange(lon_total, dtype=jnp.int32)
    cos_waves = jnp.arange(half_circle + 1, dtype=jnp.int32)
    sin_waves = jnp.arange(1, half_circle, dtype=jnp.int32)
    cos_phase = points[:, None] * cos_waves[None, :] % lon_total
    sin_phase = points[:, None] * sin_waves[None, :] % lon_total
    basis = jnp.concatenate(
        [
            jnp.cos(2.0 * math.pi * cos_phase.astype(jnp.float32) / lon_total),
            jnp.sin(2.0 * math.pi * sin_phase.astype(jnp.float32) / lon_total),
        ],
        axis=1,
    )
    waves_all = jnp.concatenate([cos_waves, sin_waves])
    wave_numbers = waves_all.astype(jnp.float32)
    weight = jnp.where(
        (waves_all == 0) | (waves_all == half_circle), 1.0 / lon_total, 2.0 / lon_total
    )
    return (basis, wave_numbers, weight)


def rim(field):
    wider = padded_2(field, (("lat", 1),), 1, False)
    return padded_2(wider, (("lon", 2),), 1, True)


def atmos_step(tracer_now, wind_u, wind_v):
    padded = rim(tracer_now)
    east_side = padded[:, 1:-1, 2:]
    west_side = padded[:, 1:-1, :-2]
    north_side = padded[:, 2:, 1:-1]
    south_side = padded[:, :-2, 1:-1]
    advect = wind_u * (east_side - west_side) + wind_v * (north_side - south_side)
    spread_sum = east_side + west_side + north_side + south_side - 4.0 * tracer_now
    return tracer_now - advect_coef * advect + diffuse_coef * spread_sum


def back_project(scaled, target_basis):
    return lax.dot_general(
        scaled,
        target_basis,
        (((1,), (1,)), ((), ())),
        precision=highest,
        preferred_element_type=jnp.float32,
    )


def ocean_step(temp, sea, air_temp, air_speed):
    top_level = temp[0] + sea * flux_coef * air_speed * (air_temp - temp[0])
    temp = jnp.concatenate([top_level[None], temp[1:]], axis=0)
    padded = rim(jnp.concatenate([temp, sea[None]], axis=0))
    level_count = temp.shape[0]
    temp_rim = padded[:level_count]
    sea_rim = padded[level_count]
    lateral = sea * (
        sea_rim[1:-1, 2:] * (temp_rim[:, 1:-1, 2:] - temp)
        + sea_rim[1:-1, :-2] * (temp_rim[:, 1:-1, :-2] - temp)
        + sea_rim[2:, 1:-1] * (temp_rim[:, 2:, 1:-1] - temp)
        + sea_rim[:-2, 1:-1] * (temp_rim[:, :-2, 1:-1] - temp)
    )
    temp = temp + ocean_diffuse * lateral
    upper = jnp.concatenate([temp[:1], temp[:-1]], axis=0)
    lower = jnp.concatenate([temp[1:], temp[-1:]], axis=0)
    return temp + vertical_mix * sea * (upper + lower - 2.0 * temp)


def per_device(tracer, wind_u, wind_v, ocean_temp, land_mask, remap_rows, remap_cols, polar_rows):
    levels, row_count, lon_local = tracer.shape
    lat_devices = lax.axis_size("lat")
    lon_devices = lax.axis_size("lon")
    lat_total = row_count * lat_devices
    lon_total = lon_local * lon_devices
    band_devices = lat_devices // 8
    band_rows = band_devices * row_count
    lat_place = lax.axis_index("lat")
    lon_place = lax.axis_index("lon")
    basis, wave_numbers, weight = make_basis(lon_total)
    own_basis = lax.dynamic_slice_in_dim(basis, lon_place * lon_local, lon_local, 0)
    own_rows = lat_place * row_count + jnp.arange(row_count, dtype=jnp.int32)
    line_count = levels * row_count
    tracer_now = tracer
    for step_index in range(STEPS):
        tracer_now = atmos_step(tracer_now, wind_u, wind_v)
        row_weights = (
            damp_table(own_rows, polar_rows, wave_numbers, lat_total, band_rows, lon_total)
            * weight[None, :]
        )
        lines = tracer_now.reshape(line_count, lon_local)
        coeffs = jnp.dot(
            lax.all_gather(lines, "lon", axis=1, tiled=True),
            basis,
            precision=highest,
            preferred_element_type=jnp.float32,
        )
        scaled = (coeffs.reshape(levels, row_count, lon_total) * row_weights[None]).reshape(
            line_count, lon_total
        )
        tracer_now = back_project(scaled, own_basis).reshape(levels, row_count, lon_local)
    bottom = jnp.stack(
        [tracer_now[levels - 1], jnp.abs(wind_u[levels - 1]) + jnp.abs(wind_v[levels - 1]) + 0.5]
    )
    bottom_rim = rim(bottom)
    local_row = remap_rows - lat_place * row_count + 1
    local_col = (remap_cols - lon_place * lon_local + 1) % lon_total
    flat_index = local_row * (lon_local + 2) + local_col
    picked = jnp.take(bottom_rim.reshape(2, -1), flat_index, axis=1)
    air_temp = picked[0]
    air_speed = picked[1]
    sea = land_mask.astype(jnp.float32)
    temp = ocean_temp
    for step_index in range(OSTEPS):
        temp = ocean_step(temp, sea, air_temp, air_speed)
    return (tracer_now, temp)


def solution(mesh):
    in_specs = (
        P(None, "lat", "lon"),
        P(None, "lat", "lon"),
        P(None, "lat", "lon"),
        P(None, "lat", "lon"),
        P("lat", "lon"),
        P("lat", "lon"),
        P("lat", "lon"),
        P(),
    )
    out_specs = (P(None, "lat", "lon"), P(None, "lat", "lon"))
    return jax.shard_map(
        per_device, mesh=mesh, in_specs=in_specs, out_specs=out_specs, check_vma=False
    )
```

profile of v0, /device:TPU:3, one launch (start us, length us, event | category | flops | bytes accessed | tf_op | source)
XLA Modules:
  0.0 390.3 jit_solution(18377480665657922847)
XLA Ops:
  7.2 1.3 fusion.94
  8.5 3.7 collective-permute-start
  12.2 8.5 %collective-permute-start.1 = (f32[32,1,288]{2,1,0:T(1,128)S(1)}, f32[32,1,288]{2,1,0:T(1,128)S(1)}, u32[]{:S(2)}, u32[]{:S(2)}) collective-permute-start(f32[32,1,288]{2,1,0:T(1,128)S(1)} %get-tuple-element.13), channel_id=1, source_target_pairs={{4,0},{8,4},{12,8},{16,12},{20,16},{24,20},{28,24},{32,28},{36,32}... | collective-permute-start | bytes 110600 | tf_op jit(solution)/shard_map/ppermute | solution.py:25
  20.7 1.1 collective-permute-done.1
  21.8 1.4 pad_maximum_fusion.34
  23.3 1.6 collective-permute-start.2
  24.9 0.4 collective-permute-start.3
  25.2 11.8 %collective-permute-done.2 = f32[32,26,1]{2,1,0:T(8,128)S(1)} collective-permute-done((f32[32,26,1]{2,1,0:T(8,128)S(1)}, f32[32,26,1]{2,1,0:T(8,128)S(1)}, u32[]{:S(2)}, u32[]{:S(2)}) %collective-permute-start.2) | collective-permute-done | bytes 3360 | tf_op jit(solution)/shard_map/ppermute | solution.py:25
  37.1 2.8 multiply_add_fusion.1
  39.8 1.3 copy.30
  41.1 0.2 all-gather.5.cloned.1.call-start
  41.7 0.2 compare_reduce_fusion
  41.8 11.0 %fusion.2 = f32[1152,577]{1,0:T(8,128)S(1)} fusion(), kind=kLoop, calls=%fused_computation.10 | loop fusion | flops 5982336 | bytes 2658816 | tf_op jit(solution)/shard_map/cos | solution.py:51
  52.9 12.6 %fusion.5 = f32[1152,575]{1,0:T(8,128)} fusion(s32[575]{0:T(1024)S(1)} %iota_add_fusion), kind=kLoop, calls=%fused_computation.13 | loop fusion | flops 5961600 | bytes 2651900 | tf_op jit(solution)/shard_map/sin | solution.py:52
  65.6 21.0 %all-gather.3.cloned.1.call-done = f32[768,1152]{0,1:T(8,128)} async-done(((f32[768,288]{0,1:T(8,128)}), f32[768,1152]{0,1:T(8,128)}) %all-gather.3.cloned.1.call-update) | async-done | bytes 3538960 | tf_op jit(solution)/shard_map/all_gather | solution.py:132
  86.5 21.0 %bitcast_multiply_fusion.1 = f32[768,1152]{1,0:T(8,128)S(1)} fusion(f32[768,1152]{0,1:T(8,128)} %all-gather.3.cloned.1.call-done, f32[1152,575]{1,0:T(8,128)} %fusion.5, f32[1152,577]{1,0:T(8,128)S(1)} %fusion.2, f32[24,1152]{1,0:T(8,128)S(1)} %fusion.87), kind=kOutput, calls=%fused_computation.5 | convolution fusion | flops 12232802304 | bytes 12496896 | tf_op jit(solution)/shard_map/dot_general | solution.py:131
  107.5 6.2 %fusion.13 = f32[32,24,288]{2,1,0:T(8,128)S(1)} fusion(f32[32,24,1152]{2,1,0:T(8,128)S(1)} %bitcast.57, s32[]{:T(128)S(6)} %select_n.72, f32[1152,577]{1,0:T(8,128)S(1)} %fusion.2, f32[1152,575]{1,0:T(8,128)S(1)} %copy-done), kind=kOutput, calls=%fused_computation.23 | convolution fusion | flops 3057979392 | bytes 9732100 | tf_op jit(solution)/shard_map/dot_general | solution.py:81
  113.8 3.3 collective-permute-start.4
  117.2 6.6 %collective-permute-start.5 = (f32[32,1,288]{2,1,0:T(1,128)S(1)}, f32[32,1,288]{2,1,0:T(1,128)S(1)}, u32[]{:S(2)}, u32[]{:S(2)}) collective-permute-start(f32[32,1,288]{2,1,0:T(1,128)S(1)} %get-tuple-element.11), channel_id=1, source_target_pairs={{4,0},{8,4},{12,8},{16,12},{20,16},{24,20},{28,24},{32,28},{36,32}... | collective-permute-start | bytes 110600 | tf_op jit(solution)/shard_map/ppermute | solution.py:25
  123.8 0.2 collective-permute-done.4
  124.0 0.9 collective-permute-done.5
  124.9 0.3 pad_maximum_fusion.31
  125.2 1.3 collective-permute-start.6
  126.5 1.0 collective-permute-start.7
  127.5 12.6 %collective-permute-done.6 = f32[32,26,1]{2,1,0:T(8,128)S(1)} collective-permute-done((f32[32,26,1]{2,1,0:T(8,128)S(1)}, f32[32,26,1]{2,1,0:T(8,128)S(1)}, u32[]{:S(2)}, u32[]{:S(2)}) %collective-permute-start.6) | collective-permute-done | bytes 3360 | tf_op jit(solution)/shard_map/ppermute | solution.py:25
  140.0 2.5 multiply_add_fusion
  142.6 2.5 copy.31
  145.4 1.1 compare_and_fusion
  146.5 0.7 reshape.175
  147.2 0.9 broadcast_clamp_fusion
  148.1 41.0 %all-gather.5.cloned.1.call-done = f32[768,1152]{0,1:T(8,128)} async-done(((f32[768,288]{0,1:T(8,128)}), f32[768,1152]{0,1:T(8,128)}) %all-gather.5.cloned.1.call-update) | async-done | bytes 3538960 | tf_op jit(solution)/shard_map/all_gather | solution.py:132
  189.1 21.0 %bitcast_multiply_fusion = f32[768,1152]{1,0:T(8,128)S(1)} fusion(f32[768,1152]{0,1:T(8,128)} %all-gather.5.cloned.1.call-done, f32[1152,575]{1,0:T(8,128)} %fusion.5, f32[1152,577]{1,0:T(8,128)S(1)} %fusion.2, f32[24,1152]{1,0:T(8,128)S(1)} %fusion.87), kind=kOutput, calls=%fused_computation.4 | convolution fusion | flops 12232802304 | bytes 12496896 | tf_op jit(solution)/shard_map/dot_general | solution.py:131
  210.0 4.1 %fusion.90 = f32[768,288]{0,1:T(8,128)S(1)} fusion(f32[768,1152]{1,0:T(8,128)S(1)} %bitcast_multiply_fusion, s32[]{:T(128)S(6)} %select_n.72, f32[1152,577]{1,0:T(8,128)S(1)} %fusion.2, f32[1152,575]{1,0:T(8,128)S(1)} %copy-done.1), kind=kOutput, calls=%fused_computation.184 | convolution fusion | flops 3057979392 | bytes 9732100 | tf_op jit(solution)/shard_map/dot_general | solution.py:81
  214.1 0.9 copy-done.6
  215.3 3.3 collective-permute-start.8
  218.6 6.6 %collective-permute-start.9 = (f32[2,1,288]{1,2,0:T(8,128)S(1)}, f32[2,1,288]{1,2,0:T(8,128)S(1)}, u32[]{:S(2)}, u32[]{:S(2)}) collective-permute-start(f32[2,1,288]{1,2,0:T(8,128)S(1)} %get-tuple-element.31), channel_id=1, source_target_pairs={{4,0},{8,4},{12,8},{16,12},{20,16},{24,20},{28,24},{32,28},{36,32}... | collective-permute-start | bytes 6920 | tf_op jit(solution)/shard_map/ppermute | solution.py:25
  225.4 5.3 %collective-permute-done.8 = f32[2,1,288]{1,2,0:T(8,128)S(1)} collective-permute-done((f32[2,1,288]{1,2,0:T(8,128)S(1)}, f32[2,1,288]{1,2,0:T(8,128)S(1)}, u32[]{:S(2)}, u32[]{:S(2)}) %collective-permute-start.8) | collective-permute-done | bytes 2336 | tf_op jit(solution)/shard_map/ppermute | solution.py:24
  230.9 0.8 collective-permute-done.9
  231.9 1.2 collective-permute-start.10
  233.2 0.9 collective-permute-done.10
  234.1 2.3 collective-permute-done.11
  236.4 0.2 pad_maximum_fusion.50
  236.8 2.7 copy.39
  239.5 97.5 %gather_fusion = f32[28672,2]{1,0:T(8,128)} fusion(f32[2,7540]{0,1:T(8,128)} %copy.39, s32[28672]{0:T(1024)S(1)} %broadcast_clamp_fusion), kind=kCustom, calls=%fused_computation | custom fusion | bytes 573440 | tf_op jit(solution)/shard_map/jit(_take)/gather | solution.py:148
  336.9 9.0 %copy.40 = f32[32,896,2]{1,0,2:T(8,128)S(1)} copy(f32[32,896,2]{2,1,0:T(8,128)} %bitcast.56) | data formatting | bytes 458752 | tf_op jit(solution)/shard_map/jit(_take)/gather | solution.py:148
  346.1 1.9 collective-permute-start.12
  348.0 9.2 %collective-permute-start.13 = (f32[5,1,896]{2,1,0:T(1,128)S(1)}, f32[5,1,896]{2,1,0:T(1,128)S(1)}, u32[]{:S(2)}, u32[]{:S(2)}) collective-permute-start(f32[5,1,896]{2,1,0:T(1,128)S(1)} %get-tuple-element.20), channel_id=1, source_target_pairs={{4,0},{8,4},{12,8},{16,12},{20,16},{24,20},{28,24},{32,28},{36,32}... | collective-permute-start | bytes 53768 | tf_op jit(solution)/shard_map/ppermute | solution.py:25
  357.3 0.9 collective-permute-done.13
  358.3 0.3 collective-permute-start.14
  358.6 0.2 collective-permute-start.15
  358.9 1.4 collective-permute-done.14
  360.3 2.7 collective-permute-done.15
  363.1 0.2 fusion.104
  363.3 0.5 fusion.29
  363.8 0.5 fusion.65
  364.6 2.1 collective-permute-start.16
  366.6 9.0 %collective-permute-start.17 = (f32[5,1,896]{2,1,0:T(1,128)S(1)}, f32[5,1,896]{2,1,0:T(1,128)S(1)}, u32[]{:S(2)}, u32[]{:S(2)}) collective-permute-start(f32[5,1,896]{2,1,0:T(1,128)S(1)} %get-tuple-element.18), channel_id=1, source_target_pairs={{4,0},{8,4},{12,8},{16,12},{20,16},{24,20},{28,24},{32,28},{36,32}... | collective-permute-start | bytes 53768 | tf_op jit(solution)/shard_map/ppermute | solution.py:25
  375.6 0.9 collective-permute-done.17
  376.6 0.4 collective-permute-start.18
  377.0 0.2 collective-permute-start.19
  377.2 1.4 copy.32
  378.7 2.4 collective-permute-done.19
  381.4 0.5 fusion.40
  382.0 1.3 fusion.68
  (76 shorter events, 3.1 us)
Async XLA Ops:
  7.2 79.3 %all-gather.3.cloned.1.call-start = ((), (), s32[]{:S(2)}) async-start(), calls=%async_computation | async-start | bytes 4423680 | tf_op jit(solution)/shard_map/all_gather | solution.py:132
  7.2 29.9 %copy-start.3 = (f32[32,24,288]{2,1,0:T(8,128)S(1)}, f32[32,24,288]{2,1,0:T(8,128)}, u32[]{:S(2)}) copy-start(f32[32,24,288]{2,1,0:T(8,128)} %param.9) | copy-start | bytes 2654212
  8.5 28.6 %copy-start.2 = (f32[32,24,288]{2,1,0:T(8,128)S(1)}, f32[32,24,288]{2,1,0:T(8,128)}, u32[]{:S(2)}) copy-start(f32[32,24,288]{2,1,0:T(8,128)} %param.8) | copy-start | bytes 2654212
  8.5 12.2 %collective-permute-start = (f32[32,1,288]{2,1,0:T(1,128)S(1)}, f32[32,1,288]{2,1,0:T(1,128)S(1)}, u32[]{:S(2)}, u32[]{:S(2)}) collective-permute-start(f32[32,1,288]{2,1,0:T(1,128)S(1)} %get-tuple-element.12), channel_id=1, source_target_pairs={{0,4},{4,8},{8,12},{12,16},{16,20},{20,24},{24,28},{28,32},{32,36}... | collective-permute-start | bytes 110600 | tf_op jit(solution)/shard_map/ppermute | solution.py:24
  12.2 9.6 %collective-permute-start.1 = (f32[32,1,288]{2,1,0:T(1,128)S(1)}, f32[32,1,288]{2,1,0:T(1,128)S(1)}, u32[]{:S(2)}, u32[]{:S(2)}) collective-permute-start(f32[32,1,288]{2,1,0:T(1,128)S(1)} %get-tuple-element.13), channel_id=1, source_target_pairs={{4,0},{8,4},{12,8},{16,12},{20,16},{24,20},{28,24},{32,28},{36,32}... | collective-permute-start | bytes 110600 | tf_op jit(solution)/shard_map/ppermute | solution.py:25
  23.3 13.8 %collective-permute-start.2 = (f32[32,26,1]{2,1,0:T(8,128)S(1)}, f32[32,26,1]{2,1,0:T(8,128)S(1)}, u32[]{:S(2)}, u32[]{:S(2)}) collective-permute-start(f32[32,26,1]{2,1,0:T(8,128)S(1)} %get-tuple-element.9), channel_id=1, source_target_pairs={{1,0},{2,1},{3,2},{0,3},{5,4},{6,5},{7,6},{4,7},{9,8},{10,9},{11,1... | collective-permute-start | bytes 9992 | tf_op jit(solution)/shard_map/ppermute | solution.py:25
  24.9 12.2 %collective-permute-start.3 = (f32[32,26,1]{2,1,0:T(8,128)S(1)}, f32[32,26,1]{2,1,0:T(8,128)S(1)}, u32[]{:S(2)}, u32[]{:S(2)}) collective-permute-start(f32[32,26,1]{2,1,0:T(8,128)S(1)} %get-tuple-element.8), channel_id=1, source_target_pairs={{0,1},{1,2},{2,3},{3,0},{4,5},{5,6},{6,7},{7,4},{8,9},{9,10},{10,1... | collective-permute-start | bytes 9992 | tf_op jit(solution)/shard_map/ppermute | solution.py:24
  39.8 1.8 copy-start.10
  41.1 147.9 %all-gather.5.cloned.1.call-start = ((), (), s32[]{:S(2)}) async-start(), calls=%async_computation.1 | async-start | bytes 4423680 | tf_op jit(solution)/shard_map/all_gather | solution.py:132
  86.5 21.0 %copy-start = (f32[1152,575]{1,0:T(8,128)S(1)}, f32[1152,575]{1,0:T(8,128)}, u32[]{:S(2)}) copy-start(f32[1152,575]{1,0:T(8,128)} %fusion.5) | copy-start | bytes 7948804
  113.7 26.3 %copy-start.5 = (f32[32,24,288]{2,1,0:T(8,128)S(1)}, f32[32,24,288]{2,1,0:T(8,128)}, u32[]{:S(2)}) copy-start(f32[32,24,288]{2,1,0:T(8,128)} %param.10) | copy-start | bytes 2654212
  113.8 26.2 %copy-start.4 = (f32[32,24,288]{2,1,0:T(8,128)S(1)}, f32[32,24,288]{2,1,0:T(8,128)}, u32[]{:S(2)}) copy-start(f32[32,24,288]{2,1,0:T(8,128)} %param.9) | copy-start | bytes 2654212
  113.8 10.2 %collective-permute-start.4 = (f32[32,1,288]{2,1,0:T(1,128)S(1)}, f32[32,1,288]{2,1,0:T(1,128)S(1)}, u32[]{:S(2)}, u32[]{:S(2)}) collective-permute-start(f32[32,1,288]{2,1,0:T(1,128)S(1)} %get-tuple-element.10), channel_id=1, source_target_pairs={{0,4},{4,8},{8,12},{12,16},{16,20},{20,24},{24,28},{28,32},{32,36}... | collective-permute-start | bytes 110600 | tf_op jit(solution)/shard_map/ppermute | solution.py:24
  117.2 7.8 %collective-permute-start.5 = (f32[32,1,288]{2,1,0:T(1,128)S(1)}, f32[32,1,288]{2,1,0:T(1,128)S(1)}, u32[]{:S(2)}, u32[]{:S(2)}) collective-permute-start(f32[32,1,288]{2,1,0:T(1,128)S(1)} %get-tuple-element.11), channel_id=1, source_target_pairs={{4,0},{8,4},{12,8},{16,12},{20,16},{24,20},{28,24},{32,28},{36,32}... | collective-permute-start | bytes 110600 | tf_op jit(solution)/shard_map/ppermute | solution.py:25
  125.2 14.8 %collective-permute-start.6 = (f32[32,26,1]{2,1,0:T(8,128)S(1)}, f32[32,26,1]{2,1,0:T(8,128)S(1)}, u32[]{:S(2)}, u32[]{:S(2)}) collective-permute-start(f32[32,26,1]{2,1,0:T(8,128)S(1)} %get-tuple-element.7), channel_id=1, source_target_pairs={{1,0},{2,1},{3,2},{0,3},{5,4},{6,5},{7,6},{4,7},{9,8},{10,9},{11,1... | collective-permute-start | bytes 9992 | tf_op jit(solution)/shard_map/ppermute | solution.py:25
  126.5 13.5 %collective-permute-start.7 = (f32[32,26,1]{2,1,0:T(8,128)S(1)}, f32[32,26,1]{2,1,0:T(8,128)S(1)}, u32[]{:S(2)}, u32[]{:S(2)}) collective-permute-start(f32[32,26,1]{2,1,0:T(8,128)S(1)} %get-tuple-element.6), channel_id=1, source_target_pairs={{0,1},{1,2},{2,3},{3,0},{4,5},{5,6},{6,7},{7,4},{8,9},{9,10},{10,1... | collective-permute-start | bytes 9992 | tf_op jit(solution)/shard_map/ppermute | solution.py:24
  142.6 2.6 slice-start
  142.6 2.7 slice-start.1
  189.1 21.0 %copy-start.1 = (f32[1152,575]{1,0:T(8,128)S(1)}, f32[1152,575]{1,0:T(8,128)}, u32[]{:S(2)}) copy-start(f32[1152,575]{1,0:T(8,128)} %fusion.5) | copy-start | bytes 7948804
  214.1 0.9 copy-start.6
  215.1 18.0 %copy-start.8 = (s32[32,896]{1,0:T(8,128)S(1)}, s32[32,896]{1,0:T(8,128)}, u32[]{:S(2)}) copy-start(s32[32,896]{1,0:T(8,128)} %param.12) | copy-start | bytes 344068
  215.3 17.9 %copy-start.9 = (f32[4,32,896]{2,1,0:T(8,128)S(1)}, f32[4,32,896]{2,1,0:T(8,128)}, u32[]{:S(2)}) copy-start(f32[4,32,896]{2,1,0:T(8,128)} %param.11) | copy-start | bytes 1376260
  215.3 15.4 %collective-permute-start.8 = (f32[2,1,288]{1,2,0:T(8,128)S(1)}, f32[2,1,288]{1,2,0:T(8,128)S(1)}, u32[]{:S(2)}, u32[]{:S(2)}) collective-permute-start(f32[2,1,288]{1,2,0:T(8,128)S(1)} %get-tuple-element.30), channel_id=1, source_target_pairs={{0,4},{4,8},{8,12},{12,16},{16,20},{20,24},{24,28},{28,32},{32,36}... | collective-permute-start | bytes 6920 | tf_op jit(solution)/shard_map/ppermute | solution.py:24
  218.6 13.0 %collective-permute-start.9 = (f32[2,1,288]{1,2,0:T(8,128)S(1)}, f32[2,1,288]{1,2,0:T(8,128)S(1)}, u32[]{:S(2)}, u32[]{:S(2)}) collective-permute-start(f32[2,1,288]{1,2,0:T(8,128)S(1)} %get-tuple-element.31), channel_id=1, source_target_pairs={{4,0},{8,4},{12,8},{16,12},{20,16},{24,20},{28,24},{32,28},{36,32}... | collective-permute-start | bytes 6920 | tf_op jit(solution)/shard_map/ppermute | solution.py:25
  231.9 2.2 collective-permute-start.10
  233.1 3.3 collective-permute-start.11
  346.1 11.2 %collective-permute-start.12 = (f32[5,1,896]{2,1,0:T(1,128)S(1)}, f32[5,1,896]{2,1,0:T(1,128)S(1)}, u32[]{:S(2)}, u32[]{:S(2)}) collective-permute-start(f32[5,1,896]{2,1,0:T(1,128)S(1)} %get-tuple-element.21), channel_id=1, source_target_pairs={{0,4},{4,8},{8,12},{12,16},{16,20},{20,24},{24,28},{28,32},{32,36}... | collective-permute-start | bytes 53768 | tf_op jit(solution)/shard_map/ppermute | solution.py:24
  348.0 10.1 %collective-permute-start.13 = (f32[5,1,896]{2,1,0:T(1,128)S(1)}, f32[5,1,896]{2,1,0:T(1,128)S(1)}, u32[]{:S(2)}, u32[]{:S(2)}) collective-permute-start(f32[5,1,896]{2,1,0:T(1,128)S(1)} %get-tuple-element.20), channel_id=1, source_target_pairs={{4,0},{8,4},{12,8},{16,12},{20,16},{24,20},{28,24},{32,28},{36,32}... | collective-permute-start | bytes 53768 | tf_op jit(solution)/shard_map/ppermute | solution.py:25
  358.3 2.0 collective-permute-start.14
  358.6 4.3 %collective-permute-start.15 = (f32[5,34,1]{2,1,0:T(8,128)S(1)}, f32[5,34,1]{2,1,0:T(8,128)S(1)}, u32[]{:S(2)}, u32[]{:S(2)}) collective-permute-start(f32[5,34,1]{2,1,0:T(8,128)S(1)} %get-tuple-element.16), channel_id=1, source_target_pairs={{1,0},{2,1},{3,2},{0,3},{5,4},{6,5},{7,6},{4,7},{9,8},{10,9},{11,1... | collective-permute-start | bytes 2048 | tf_op jit(solution)/shard_map/ppermute | solution.py:25
  364.5 12.7 %copy-start.7 = (f32[768,288]{0,1:T(8,128)S(1)}, f32[768,288]{0,1:T(8,128)}, u32[]{:S(2)}) copy-start(f32[768,288]{0,1:T(8,128)} %copy-done.6) | copy-start | bytes 2654212
  364.6 11.0 %collective-permute-start.16 = (f32[5,1,896]{2,1,0:T(1,128)S(1)}, f32[5,1,896]{2,1,0:T(1,128)S(1)}, u32[]{:S(2)}, u32[]{:S(2)}) collective-permute-start(f32[5,1,896]{2,1,0:T(1,128)S(1)} %get-tuple-element.19), channel_id=1, source_target_pairs={{0,4},{4,8},{8,12},{12,16},{16,20},{20,24},{24,28},{28,32},{32,36}... | collective-permute-start | bytes 53768 | tf_op jit(solution)/shard_map/ppermute | solution.py:24
  366.6 9.8 %collective-permute-start.17 = (f32[5,1,896]{2,1,0:T(1,128)S(1)}, f32[5,1,896]{2,1,0:T(1,128)S(1)}, u32[]{:S(2)}, u32[]{:S(2)}) collective-permute-start(f32[5,1,896]{2,1,0:T(1,128)S(1)} %get-tuple-element.18), channel_id=1, source_target_pairs={{4,0},{8,4},{12,8},{16,12},{20,16},{24,20},{28,24},{32,28},{36,32}... | collective-permute-start | bytes 53768 | tf_op jit(solution)/shard_map/ppermute | solution.py:25
  376.6 2.1 collective-permute-start.18
  377.0 4.1 %collective-permute-start.19 = (f32[5,34,1]{2,1,0:T(8,128)S(1)}, f32[5,34,1]{2,1,0:T(8,128)S(1)}, u32[]{:S(2)}, u32[]{:S(2)}) collective-permute-start(f32[5,34,1]{2,1,0:T(8,128)S(1)} %get-tuple-element.14), channel_id=1, source_target_pairs={{1,0},{2,1},{3,2},{0,3},{5,4},{6,5},{7,6},{4,7},{9,8},{10,9},{11,1... | collective-permute-start | bytes 2048 | tf_op jit(solution)/shard_map/ppermute | solution.py:25
Sparse Core Ops, SparseCore 0:
  41.2 45.2 all-gather.2
  145.3 43.7 all-gather.4
where the time goes:
time: 394 us; the launch traced here: 390 us
  local copies, waits for them, and re-layouts  119 us (30%)
  waiting for transfers between devices  106 us (27%)
  starting transfers between devices  61 us (15%)
  matrix products  52.2 us (13%)
  other arithmetic  37 us (9%)
  between operations  14.9 us (4%)
    gather x2, local copies, waits for them, and re-layouts, per_device(): picked = jnp.take(bottom_rim.reshape(2, -1), flat_index, axis=1)  106 us
    all_gather x2, waiting for transfers between devices, per_device(): lax.all_gather(lines, 'lon', axis=1, tiled=True)  61.9 us
    ppermute x10, starting transfers between devices, padded_2(): after = lax.ppermute(first, axis, down)  43.2 us
    dot_general x2, matrix products, per_device(): jnp.dot(lax.all_gather(lines, 'lon', axis=1, tiled=True), basis, precisio...  41.9 us
    ppermute x10, waiting for transfers between devices, padded_2(): after = lax.ppermute(first, axis, down)  36.3 us
    ppermute x10, starting transfers between devices, padded_2(): before = lax.ppermute(last, axis, up)  17.6 us
    sin x1, other arithmetic, make_basis(): jnp.sin(2.0 * math.pi * sin_phase.astype(jnp.float32) / lon_total)  12.6 us
    cos x1, other arithmetic, make_basis(): jnp.cos(2.0 * math.pi * cos_phase.astype(jnp.float32) / lon_total)  11 us
  transfers between devices with their start and end apart: 22, of which 17 were waited for; matrix products, arithmetic and copies ran while one was open for 7% of the time, Pallas kernels for 0%

commit v1 on v0

--- a/solution.py
+++ b/solution.py
@@ -12,6 +12,11 @@
 ocean_diffuse = 0.15
 vertical_mix = 0.2
 highest = lax.Precision.HIGHEST
+
+
+def exchange_gather(x, axis, dim):
+    outgoing = jnp.stack([x] * lax.axis_size(axis))
+    return jnp.concatenate(lax.all_to_all(outgoing, axis, 0, 0), axis=dim)
 
 
 def padded_2(shard, sides, width, wrap):
@@ -129,7 +134,7 @@
         )
         lines = tracer_now.reshape(line_count, lon_local)
         coeffs = jnp.dot(
-            lax.all_gather(lines, "lon", axis=1, tiled=True),
+            exchange_gather(lines, "lon", 1),
             basis,
             precision=highest,
             preferred_element_type=jnp.float32,

time: 394 us -> 411 us (1.043)
  local copies, waits for them, and re-layouts: 119 us -> 146 us
  starting transfers between devices: 61 us -> 76.1 us
  between operations: 14.9 us -> 1.56 us
  waiting for transfers between devices: 106 us -> 97.8 us
    all_gather x2 -> x0, waiting for transfers between devices: 61.9 us -> none  [per_device(): lax.all_gather(lines, 'lon', axis=1, tiled=True)]
    all_to_all x0 -> x2, waiting for transfers between devices: none -> 55.3 us  [exchange_gather(): return jnp.concatenate(lax.all_to_all(outgoing, axis, 0, 0), axis=dim)]
    all_to_all x0 -> x2, starting transfers between devices: none -> 12.9 us  [exchange_gather(): return jnp.concatenate(lax.all_to_all(outgoing, axis, 0, 0), axis=dim)]
    dot_general x0 -> x2, local copies, waits for them, and re-layouts: none -> 11.8 us  [per_device(): jnp.dot(exchange_gather(lines, 'lon', 1), basis, precision=highest, prefe...]
    reshape x2, local copies, waits for them, and re-layouts: 3.8 us -> 12.5 us  [exchange_gather(): return jnp.concatenate(lax.all_to_all(outgoing, axis, 0, 0), axis=dim)]
    another operation x0 -> x4, local copies, waits for them, and re-layouts: none -> 8.11 us  [exchange_gather(): outgoing = jnp.stack([x] * lax.axis_size(axis))]
    ppermute x10, starting transfers between devices: 43.2 us -> 48.8 us  [padded_2(): after = lax.ppermute(first, axis, down)]
  transfers between devices with their start and end apart: 22 -> 22, of which waited for: 17 -> 16; matrix products, arithmetic and copies ran while one was open for 7% -> 7% of each run, Pallas kernels for 0% -> 0%
where the time goes in v1:
time: 411 us; the launch traced here: 406 us
  local copies, waits for them, and re-layouts  146 us (36%)
  waiting for transfers between devices  97.8 us (24%)
  starting transfers between devices  76.1 us (19%)
  matrix products  48.7 us (12%)
  other arithmetic  35.6 us (9%)
    gather x2, local copies, waits for them, and re-layouts, per_device(): picked = jnp.take(bottom_rim.reshape(2, -1), flat_index, axis=1)  106 us
    all_to_all x2, waiting for transfers between devices, exchange_gather(): return jnp.concatenate(lax.all_to_all(outgoing, axis, 0, 0), axis=dim)  55.3 us
    ppermute x10, starting transfers between devices, padded_2(): after = lax.ppermute(first, axis, down)  48.8 us
    dot_general x2, matrix products, per_device(): jnp.dot(exchange_gather(lines, 'lon', 1), basis, precision=highest, prefe...  38.4 us
    ppermute x10, waiting for transfers between devices, padded_2(): after = lax.ppermute(first, axis, down)  36.4 us
    ppermute x10, starting transfers between devices, padded_2(): before = lax.ppermute(last, axis, up)  14.3 us
    all_to_all x2, starting transfers between devices, exchange_gather(): return jnp.concatenate(lax.all_to_all(outgoing, axis, 0, 0), axis=dim)  12.9 us
    reshape x2, local copies, waits for them, and re-layouts, exchange_gather(): return jnp.concatenate(lax.all_to_all(outgoing, axis, 0, 0), axis=dim)  12.5 us
  transfers between devices with their start and end apart: 22, of which 16 were waited for; matrix products, arithmetic and copies ran while one was open for 7% of the time, Pallas kernels for 0%

profile of v1, /device:TPU:3, one launch (start us, length us, event | category | flops | bytes accessed | tf_op | source)
XLA Modules:
  0.0 406.1 jit_solution(1494458569131659530)
XLA Ops:
  0.7 1.3 fusion.97
  2.0 3.5 collective-permute-start
  5.5 8.5 %collective-permute-start.1 = (f32[32,1,288]{2,1,0:T(1,128)S(1)}, f32[32,1,288]{2,1,0:T(1,128)S(1)}, u32[]{:S(2)}, u32[]{:S(2)}) collective-permute-start(f32[32,1,288]{2,1,0:T(1,128)S(1)} %get-tuple-element.13), channel_id=1, source_target_pairs={{4,0},{8,4},{12,8},{16,12},{20,16},{24,20},{28,24},{32,28},{36,32}... | collective-permute-start | bytes 110600 | tf_op jit(solution)/shard_map/ppermute | solution.py:30
  14.0 1.1 collective-permute-done.1
  15.2 1.4 pad_maximum_fusion.32
  16.6 1.6 collective-permute-start.2
  18.2 0.4 collective-permute-start.3
  18.6 11.8 %collective-permute-done.2 = f32[32,26,1]{2,1,0:T(8,128)S(1)} collective-permute-done((f32[32,26,1]{2,1,0:T(8,128)S(1)}, f32[32,26,1]{2,1,0:T(8,128)S(1)}, u32[]{:S(2)}, u32[]{:S(2)}) %collective-permute-start.2) | collective-permute-done | bytes 3360 | tf_op jit(solution)/shard_map/ppermute | solution.py:30
  30.4 2.8 multiply_add_fusion.1
  33.2 0.3 copy.32
  33.5 2.1 stack.10
  35.6 6.6 %all-to-all-start = ((f32[4,768,288]{1,2,0:T(8,128)}), f32[4,768,288]{1,2,0:T(8,128)}, u32[]{:S(2)}, u32[]{:S(2)}) async-start(f32[4,768,288]{1,2,0:T(8,128)} %stack.10), calls=%async_computation | async-start | bytes 7077888 | tf_op jit(solution)/shard_map/all_to_all | solution.py:19
  42.7 11.0 %fusion.5 = f32[1152,577]{1,0:T(8,128)S(1)} fusion(), kind=kLoop, calls=%fused_computation.11 | loop fusion | flops 5982336 | bytes 2658816 | tf_op jit(solution)/shard_map/cos | solution.py:56
  53.8 12.2 %fusion.8 = f32[1152,575]{1,0:T(8,128)} fusion(s32[575]{0:T(1024)S(1)} %iota_add_fusion), kind=kLoop, calls=%fused_computation.14 | loop fusion | flops 5961600 | bytes 2651900 | tf_op jit(solution)/shard_map/sin | solution.py:57
  66.0 16.4 %all-to-all-done = f32[4,768,288]{1,2,0:T(8,128)} async-done(((f32[4,768,288]{1,2,0:T(8,128)}), f32[4,768,288]{1,2,0:T(8,128)}, u32[]{:S(2)}, u32[]{:S(2)}) %all-to-all-start) | async-done | bytes 3538976 | tf_op jit(solution)/shard_map/all_to_all | solution.py:19
  82.4 6.3 %copy.33 = f32[768,4,288]{2,1,0:T(4,128)} copy(f32[768,4,288]{0,2,1:T(8,128)} %bitcast.1) | data formatting | bytes 7077888 | tf_op jit(solution)/shard_map/reshape | solution.py:19
  88.6 5.9 %dot_general.16 = f32[32,24,1152]{2,1,0:T(8,128)} reshape(f32[768,4,288]{2,1,0:T(4,128)} %copy.33) | data formatting | bytes 7077888 | tf_op jit(solution)/shard_map/dot_general | solution.py:136
  94.6 19.3 %convolution_multiply_fusion.1 = f32[32,24,1152]{2,1,0:T(8,128)S(1)} fusion(f32[32,24,1152]{2,1,0:T(8,128)} %dot_general.16, f32[1152,575]{1,0:T(8,128)} %fusion.8, f32[1152,577]{1,0:T(8,128)S(1)} %fusion.5, f32[24,1152]{1,0:T(8,128)S(1)} %fusion.90), kind=kOutput, calls=%fused_computation.8 | convolution fusion | flops 12232802304 | bytes 12496896 | tf_op jit(solution)/shard_map/dot_general | solution.py:136
  113.9 6.2 %fusion.16 = f32[32,24,288]{2,1,0:T(8,128)S(1)} fusion(f32[32,24,1152]{2,1,0:T(8,128)S(1)} %convolution_multiply_fusion.1, s32[]{:T(128)S(6)} %select_n.72, f32[1152,577]{1,0:T(8,128)S(1)} %fusion.5, f32[1152,575]{1,0:T(8,128)S(1)} %copy-done), kind=kOutput, calls=%fused_computation.24 | convolution fusion | flops 3057979392 | bytes 9732100 | tf_op jit(solution)/shard_map/dot_general | solution.py:86
  120.2 2.1 collective-permute-start.4
  122.3 9.1 %collective-permute-start.5 = (f32[32,1,288]{2,1,0:T(1,128)S(1)}, f32[32,1,288]{2,1,0:T(1,128)S(1)}, u32[]{:S(2)}, u32[]{:S(2)}) collective-permute-start(f32[32,1,288]{2,1,0:T(1,128)S(1)} %get-tuple-element.11), channel_id=1, source_target_pairs={{4,0},{8,4},{12,8},{16,12},{20,16},{24,20},{28,24},{32,28},{36,32}... | collective-permute-start | bytes 110600 | tf_op jit(solution)/shard_map/ppermute | solution.py:30
  131.4 1.1 collective-permute-done.5
  132.8 1.9 collective-permute-start.6
  134.8 11.4 %collective-permute-done.6 = f32[32,26,1]{2,1,0:T(8,128)S(1)} collective-permute-done((f32[32,26,1]{2,1,0:T(8,128)S(1)}, f32[32,26,1]{2,1,0:T(8,128)S(1)}, u32[]{:S(2)}, u32[]{:S(2)}) %collective-permute-start.6) | collective-permute-done | bytes 3360 | tf_op jit(solution)/shard_map/ppermute | solution.py:30
  146.3 2.5 multiply_add_fusion
  148.8 2.5 copy.34
  151.4 3.2 stack.11
  154.6 6.3 %all-to-all-start.1 = ((f32[4,768,288]{1,2,0:T(8,128)}), f32[4,768,288]{1,2,0:T(8,128)}, u32[]{:S(2)}, u32[]{:S(2)}) async-start(f32[4,768,288]{1,2,0:T(8,128)} %stack.11), calls=%async_computation.1 | async-start | bytes 7077888 | tf_op jit(solution)/shard_map/all_to_all | solution.py:19
  161.1 1.0 compare_and_fusion
  162.2 38.9 %all-to-all-done.1 = f32[4,768,288]{1,2,0:T(8,128)} async-done(((f32[4,768,288]{1,2,0:T(8,128)}), f32[4,768,288]{1,2,0:T(8,128)}, u32[]{:S(2)}, u32[]{:S(2)}) %all-to-all-start.1) | async-done | bytes 3538976 | tf_op jit(solution)/shard_map/all_to_all | solution.py:19
  201.2 6.3 %copy.35 = f32[768,4,288]{2,1,0:T(4,128)} copy(f32[768,4,288]{0,2,1:T(8,128)} %bitcast.5) | data formatting | bytes 7077888 | tf_op jit(solution)/shard_map/reshape | solution.py:19
  207.4 5.9 %dot_general.19 = f32[32,24,1152]{2,1,0:T(8,128)} reshape(f32[768,4,288]{2,1,0:T(4,128)} %copy.35) | data formatting | bytes 7077888 | tf_op jit(solution)/shard_map/dot_general | solution.py:136
  213.4 19.1 %convolution_multiply_fusion = f32[32,24,1152]{2,1,0:T(8,128)S(1)} fusion(f32[32,24,1152]{2,1,0:T(8,128)} %dot_general.19, f32[1152,575]{1,0:T(8,128)} %fusion.8, f32[1152,577]{1,0:T(8,128)S(1)} %fusion.5, f32[24,1152]{1,0:T(8,128)S(1)} %copy-done.12), kind=kOutput, calls=%fused_computation.7 | convolution fusion | flops 12232802304 | bytes 12496896 | tf_op jit(solution)/shard_map/dot_general | solution.py:136
  232.5 4.1 %fusion.93 = f32[768,288]{0,1:T(8,128)S(1)} fusion(f32[768,1152]{1,0:T(8,128)S(1)} %bitcast.62, s32[]{:T(128)S(6)} %select_n.72, f32[1152,577]{1,0:T(8,128)S(1)} %fusion.5, f32[1152,575]{1,0:T(8,128)S(1)} %copy-done.1), kind=kOutput, calls=%fused_computation.185 | convolution fusion | flops 3057979392 | bytes 9732100 | tf_op jit(solution)/shard_map/dot_general | solution.py:86
  236.6 0.9 copy-done.6
  237.8 2.1 collective-permute-start.8
  239.9 8.6 %collective-permute-start.9 = (f32[2,1,288]{1,2,0:T(8,128)S(1)}, f32[2,1,288]{1,2,0:T(8,128)S(1)}, u32[]{:S(2)}, u32[]{:S(2)}) collective-permute-start(f32[2,1,288]{1,2,0:T(8,128)S(1)} %get-tuple-element.31), channel_id=1, source_target_pairs={{4,0},{8,4},{12,8},{16,12},{20,16},{24,20},{28,24},{32,28},{36,32}... | collective-permute-start | bytes 6920 | tf_op jit(solution)/shard_map/ppermute | solution.py:30
  248.6 4.3 %collective-permute-done.8 = f32[2,1,288]{1,2,0:T(8,128)S(1)} collective-permute-done((f32[2,1,288]{1,2,0:T(8,128)S(1)}, f32[2,1,288]{1,2,0:T(8,128)S(1)}, u32[]{:S(2)}, u32[]{:S(2)}) %collective-permute-start.8) | collective-permute-done | bytes 2336 | tf_op jit(solution)/shard_map/ppermute | solution.py:29
  253.0 0.8 collective-permute-done.9
  254.1 1.7 collective-permute-start.10
  255.7 0.3 collective-permute-start.11
  256.1 0.6 collective-permute-done.10
  256.7 2.3 collective-permute-done.11
  259.3 2.7 copy.43
  262.0 96.8 %gather_fusion = f32[28672,2]{1,0:T(8,128)} fusion(f32[2,7540]{0,1:T(8,128)} %copy.43, s32[28672]{0:T(1024)S(1)} %broadcast_clamp_fusion), kind=kCustom, calls=%fused_computation | custom fusion | bytes 573440 | tf_op jit(solution)/shard_map/jit(_take)/gather | solution.py:153
  358.8 9.0 %copy.44 = f32[32,896,2]{1,0,2:T(8,128)S(1)} copy(f32[32,896,2]{2,1,0:T(8,128)} %bitcast.59) | data formatting | bytes 458752 | tf_op jit(solution)/shard_map/jit(_take)/gather | solution.py:153
  368.0 1.9 collective-permute-start.12
  369.9 9.2 %collective-permute-start.13 = (f32[5,1,896]{2,1,0:T(1,128)S(1)}, f32[5,1,896]{2,1,0:T(1,128)S(1)}, u32[]{:S(2)}, u32[]{:S(2)}) collective-permute-start(f32[5,1,896]{2,1,0:T(1,128)S(1)} %get-tuple-element.20), channel_id=1, source_target_pairs={{4,0},{8,4},{12,8},{16,12},{20,16},{24,20},{28,24},{32,28},{36,32}... | collective-permute-start | bytes 53768 | tf_op jit(solution)/shard_map/ppermute | solution.py:30
  379.2 0.9 collective-permute-done.13
  380.2 0.3 collective-permute-start.14
  380.5 0.6 collective-permute-start.15
  381.1 1.1 collective-permute-done.14
  382.2 3.1 collective-permute-done.15
  385.6 0.5 fusion.32
  386.1 0.5 fusion.68
  386.9 2.1 collective-permute-start.16
  388.9 8.6 %collective-permute-start.17 = (f32[5,1,896]{2,1,0:T(1,128)S(1)}, f32[5,1,896]{2,1,0:T(1,128)S(1)}, u32[]{:S(2)}, u32[]{:S(2)}) collective-permute-start(f32[5,1,896]{2,1,0:T(1,128)S(1)} %get-tuple-element.18), channel_id=1, source_target_pairs={{4,0},{8,4},{12,8},{16,12},{20,16},{24,20},{28,24},{32,28},{36,32}... | collective-permute-start | bytes 53768 | tf_op jit(solution)/shard_map/ppermute | solution.py:30
  397.5 0.9 collective-permute-done.17
  398.6 0.3 collective-permute-start.18
  398.9 0.4 collective-permute-start.19
  399.3 1.4 copy.36
  400.7 3.0 collective-permute-done.19
  404.0 0.5 fusion.43
  404.6 1.3 fusion.71
  (86 shorter events, 3.8 us)
Async XLA Ops:
  0.6 29.8 %copy-start.2 = (f32[32,24,288]{2,1,0:T(8,128)S(1)}, f32[32,24,288]{2,1,0:T(8,128)}, u32[]{:S(2)}) copy-start(f32[32,24,288]{2,1,0:T(8,128)} %param.8) | copy-start | bytes 2654212
  0.6 29.8 %copy-start.3 = (f32[32,24,288]{2,1,0:T(8,128)S(1)}, f32[32,24,288]{2,1,0:T(8,128)}, u32[]{:S(2)}) copy-start(f32[32,24,288]{2,1,0:T(8,128)} %param.9) | copy-start | bytes 2654212
  2.0 12.0 %collective-permute-start = (f32[32,1,288]{2,1,0:T(1,128)S(1)}, f32[32,1,288]{2,1,0:T(1,128)S(1)}, u32[]{:S(2)}, u32[]{:S(2)}) collective-permute-start(f32[32,1,288]{2,1,0:T(1,128)S(1)} %get-tuple-element.12), channel_id=1, source_target_pairs={{0,4},{4,8},{8,12},{12,16},{16,20},{20,24},{24,28},{28,32},{32,36}... | collective-permute-start | bytes 110600 | tf_op jit(solution)/shard_map/ppermute | solution.py:29
  5.5 9.6 %collective-permute-start.1 = (f32[32,1,288]{2,1,0:T(1,128)S(1)}, f32[32,1,288]{2,1,0:T(1,128)S(1)}, u32[]{:S(2)}, u32[]{:S(2)}) collective-permute-start(f32[32,1,288]{2,1,0:T(1,128)S(1)} %get-tuple-element.13), channel_id=1, source_target_pairs={{4,0},{8,4},{12,8},{16,12},{20,16},{24,20},{28,24},{32,28},{36,32}... | collective-permute-start | bytes 110600 | tf_op jit(solution)/shard_map/ppermute | solution.py:30
  16.6 13.8 %collective-permute-start.2 = (f32[32,26,1]{2,1,0:T(8,128)S(1)}, f32[32,26,1]{2,1,0:T(8,128)S(1)}, u32[]{:S(2)}, u32[]{:S(2)}) collective-permute-start(f32[32,26,1]{2,1,0:T(8,128)S(1)} %get-tuple-element.9), channel_id=1, source_target_pairs={{1,0},{2,1},{3,2},{0,3},{5,4},{6,5},{7,6},{4,7},{9,8},{10,9},{11,1... | collective-permute-start | bytes 9992 | tf_op jit(solution)/shard_map/ppermute | solution.py:30
  18.2 12.2 %collective-permute-start.3 = (f32[32,26,1]{2,1,0:T(8,128)S(1)}, f32[32,26,1]{2,1,0:T(8,128)S(1)}, u32[]{:S(2)}, u32[]{:S(2)}) collective-permute-start(f32[32,26,1]{2,1,0:T(8,128)S(1)} %get-tuple-element.8), channel_id=1, source_target_pairs={{0,1},{1,2},{2,3},{3,0},{4,5},{5,6},{6,7},{7,4},{8,9},{9,10},{10,1... | collective-permute-start | bytes 9992 | tf_op jit(solution)/shard_map/ppermute | solution.py:29
  35.6 6.9 %copy-start.13 = (s32[192]{0:T(256)S(1)}, s32[192]{0:T(256)}, u32[]{:S(2)}) copy-start(s32[192]{0:T(256)} %param.15) | copy-start | bytes 2308
  35.6 46.8 %all-to-all-start = ((f32[4,768,288]{1,2,0:T(8,128)}), f32[4,768,288]{1,2,0:T(8,128)}, u32[]{:S(2)}, u32[]{:S(2)}) async-start(f32[4,768,288]{1,2,0:T(8,128)} %stack.10), calls=%async_computation | async-start | bytes 7077888 | tf_op jit(solution)/shard_map/all_to_all | solution.py:19
  53.8 40.8 %copy-start.11 = (f32[24,1152]{1,0:T(8,128)}, f32[24,1152]{1,0:T(8,128)S(1)}, u32[]{:S(2)}) copy-start(f32[24,1152]{1,0:T(8,128)S(1)} %fusion.90) | copy-start | bytes 331780
  94.6 19.3 %copy-start = (f32[1152,575]{1,0:T(8,128)S(1)}, f32[1152,575]{1,0:T(8,128)}, u32[]{:S(2)}) copy-start(f32[1152,575]{1,0:T(8,128)} %fusion.8) | copy-start | bytes 7948804
  120.1 26.2 %copy-start.4 = (f32[32,24,288]{2,1,0:T(8,128)S(1)}, f32[32,24,288]{2,1,0:T(8,128)}, u32[]{:S(2)}) copy-start(f32[32,24,288]{2,1,0:T(8,128)} %param.9) | copy-start | bytes 2654212
  120.2 26.2 %copy-start.5 = (f32[32,24,288]{2,1,0:T(8,128)S(1)}, f32[32,24,288]{2,1,0:T(8,128)}, u32[]{:S(2)}) copy-start(f32[32,24,288]{2,1,0:T(8,128)} %param.10) | copy-start | bytes 2654212
  120.2 11.2 %collective-permute-start.4 = (f32[32,1,288]{2,1,0:T(1,128)S(1)}, f32[32,1,288]{2,1,0:T(1,128)S(1)}, u32[]{:S(2)}, u32[]{:S(2)}) collective-permute-start(f32[32,1,288]{2,1,0:T(1,128)S(1)} %get-tuple-element.10), channel_id=1, source_target_pairs={{0,4},{4,8},{8,12},{12,16},{16,20},{20,24},{24,28},{28,32},{32,36}... | collective-permute-start | bytes 110600 | tf_op jit(solution)/shard_map/ppermute | solution.py:29
  122.3 10.2 %collective-permute-start.5 = (f32[32,1,288]{2,1,0:T(1,128)S(1)}, f32[32,1,288]{2,1,0:T(1,128)S(1)}, u32[]{:S(2)}, u32[]{:S(2)}) collective-permute-start(f32[32,1,288]{2,1,0:T(1,128)S(1)} %get-tuple-element.11), channel_id=1, source_target_pairs={{4,0},{8,4},{12,8},{16,12},{20,16},{24,20},{28,24},{32,28},{36,32}... | collective-permute-start | bytes 110600 | tf_op jit(solution)/shard_map/ppermute | solution.py:30
  132.8 13.4 %collective-permute-start.6 = (f32[32,26,1]{2,1,0:T(8,128)S(1)}, f32[32,26,1]{2,1,0:T(8,128)S(1)}, u32[]{:S(2)}, u32[]{:S(2)}) collective-permute-start(f32[32,26,1]{2,1,0:T(8,128)S(1)} %get-tuple-element.7), channel_id=1, source_target_pairs={{1,0},{2,1},{3,2},{0,3},{5,4},{6,5},{7,6},{4,7},{9,8},{10,9},{11,1... | collective-permute-start | bytes 9992 | tf_op jit(solution)/shard_map/ppermute | solution.py:30
  134.8 11.6 %collective-permute-start.7 = (f32[32,26,1]{2,1,0:T(8,128)S(1)}, f32[32,26,1]{2,1,0:T(8,128)S(1)}, u32[]{:S(2)}, u32[]{:S(2)}) collective-permute-start(f32[32,26,1]{2,1,0:T(8,128)S(1)} %get-tuple-element.6), channel_id=1, source_target_pairs={{0,1},{1,2},{2,3},{3,0},{4,5},{5,6},{6,7},{7,4},{8,9},{9,10},{10,1... | collective-permute-start | bytes 9992 | tf_op jit(solution)/shard_map/ppermute | solution.py:29
  154.6 6.3 %slice-start = ((f32[32,24,288]{2,1,0:T(8,128)}), f32[1,24,288]{2,1,0:T(8,128)S(1)}, s32[]{:S(2)}) async-start(f32[32,24,288]{2,1,0:T(8,128)} %param.9), calls=%async_computation.2 | async-start | bytes 73728 | tf_op jit(solution)/shard_map/slice | solution.py:147
  154.6 6.4 %slice-start.1 = ((f32[32,24,288]{2,1,0:T(8,128)}), f32[1,24,288]{2,1,0:T(8,128)S(1)}, s32[]{:S(2)}) async-start(f32[32,24,288]{2,1,0:T(8,128)} %param.10), calls=%async_computation.3 | async-start | bytes 73728 | tf_op jit(solution)/shard_map/slice | solution.py:147
  154.6 6.6 %copy-start.10 = (s32[32,896]{1,0:T(8,128)S(1)}, s32[32,896]{1,0:T(8,128)}, u32[]{:S(2)}) copy-start(s32[32,896]{1,0:T(8,128)} %param.14) | copy-start | bytes 344068
  154.6 46.6 %all-to-all-start.1 = ((f32[4,768,288]{1,2,0:T(8,128)}), f32[4,768,288]{1,2,0:T(8,128)}, u32[]{:S(2)}, u32[]{:S(2)}) async-start(f32[4,768,288]{1,2,0:T(8,128)} %stack.11), calls=%async_computation.1 | async-start | bytes 7077888 | tf_op jit(solution)/shard_map/all_to_all | solution.py:19
  207.4 5.9 %copy-start.12 = (f32[24,1152]{1,0:T(8,128)S(1)}, f32[24,1152]{1,0:T(8,128)}, u32[]{:S(2)}) copy-start(f32[24,1152]{1,0:T(8,128)} %copy-done.11) | copy-start | bytes 331780
  213.4 19.1 %copy-start.1 = (f32[1152,575]{1,0:T(8,128)S(1)}, f32[1152,575]{1,0:T(8,128)}, u32[]{:S(2)}) copy-start(f32[1152,575]{1,0:T(8,128)} %fusion.8) | copy-start | bytes 7948804
  236.6 0.9 copy-start.6
  237.6 18.4 %copy-start.8 = (s32[32,896]{1,0:T(8,128)S(1)}, s32[32,896]{1,0:T(8,128)}, u32[]{:S(2)}) copy-start(s32[32,896]{1,0:T(8,128)} %param.12) | copy-start | bytes 344068
  237.6 18.4 %copy-start.9 = (f32[4,32,896]{2,1,0:T(8,128)S(1)}, f32[4,32,896]{2,1,0:T(8,128)}, u32[]{:S(2)}) copy-start(f32[4,32,896]{2,1,0:T(8,128)} %param.11) | copy-start | bytes 1376260
  237.8 15.1 %collective-permute-start.8 = (f32[2,1,288]{1,2,0:T(8,128)S(1)}, f32[2,1,288]{1,2,0:T(8,128)S(1)}, u32[]{:S(2)}, u32[]{:S(2)}) collective-permute-start(f32[2,1,288]{1,2,0:T(8,128)S(1)} %get-tuple-element.30), channel_id=1, source_target_pairs={{0,4},{4,8},{8,12},{12,16},{16,20},{20,24},{24,28},{28,32},{32,36}... | collective-permute-start | bytes 6920 | tf_op jit(solution)/shard_map/ppermute | solution.py:29
  239.9 13.9 %collective-permute-start.9 = (f32[2,1,288]{1,2,0:T(8,128)S(1)}, f32[2,1,288]{1,2,0:T(8,128)S(1)}, u32[]{:S(2)}, u32[]{:S(2)}) collective-permute-start(f32[2,1,288]{1,2,0:T(8,128)S(1)} %get-tuple-element.31), channel_id=1, source_target_pairs={{4,0},{8,4},{12,8},{16,12},{20,16},{24,20},{28,24},{32,28},{36,32}... | collective-permute-start | bytes 6920 | tf_op jit(solution)/shard_map/ppermute | solution.py:30
  254.1 2.6 collective-permute-start.10
  255.7 3.3 collective-permute-start.11
  368.0 11.2 %collective-permute-start.12 = (f32[5,1,896]{2,1,0:T(1,128)S(1)}, f32[5,1,896]{2,1,0:T(1,128)S(1)}, u32[]{:S(2)}, u32[]{:S(2)}) collective-permute-start(f32[5,1,896]{2,1,0:T(1,128)S(1)} %get-tuple-element.21), channel_id=1, source_target_pairs={{0,4},{4,8},{8,12},{12,16},{16,20},{20,24},{24,28},{28,32},{32,36}... | collective-permute-start | bytes 53768 | tf_op jit(solution)/shard_map/ppermute | solution.py:29
  369.9 10.1 %collective-permute-start.13 = (f32[5,1,896]{2,1,0:T(1,128)S(1)}, f32[5,1,896]{2,1,0:T(1,128)S(1)}, u32[]{:S(2)}, u32[]{:S(2)}) collective-permute-start(f32[5,1,896]{2,1,0:T(1,128)S(1)} %get-tuple-element.20), channel_id=1, source_target_pairs={{4,0},{8,4},{12,8},{16,12},{20,16},{24,20},{28,24},{32,28},{36,32}... | collective-permute-start | bytes 53768 | tf_op jit(solution)/shard_map/ppermute | solution.py:30
  380.2 2.0 collective-permute-start.14
  380.5 4.7 %collective-permute-start.15 = (f32[5,34,1]{2,1,0:T(8,128)S(1)}, f32[5,34,1]{2,1,0:T(8,128)S(1)}, u32[]{:S(2)}, u32[]{:S(2)}) collective-permute-start(f32[5,34,1]{2,1,0:T(8,128)S(1)} %get-tuple-element.16), channel_id=1, source_target_pairs={{1,0},{2,1},{3,2},{0,3},{5,4},{6,5},{7,6},{4,7},{9,8},{10,9},{11,1... | collective-permute-start | bytes 2048 | tf_op jit(solution)/shard_map/ppermute | solution.py:30
  386.8 12.6 %copy-start.7 = (f32[768,288]{0,1:T(8,128)S(1)}, f32[768,288]{0,1:T(8,128)}, u32[]{:S(2)}) copy-start(f32[768,288]{0,1:T(8,128)} %copy-done.6) | copy-start | bytes 2654212
  386.9 10.7 %collective-permute-start.16 = (f32[5,1,896]{2,1,0:T(1,128)S(1)}, f32[5,1,896]{2,1,0:T(1,128)S(1)}, u32[]{:S(2)}, u32[]{:S(2)}) collective-permute-start(f32[5,1,896]{2,1,0:T(1,128)S(1)} %get-tuple-element.19), channel_id=1, source_target_pairs={{0,4},{4,8},{8,12},{12,16},{16,20},{20,24},{24,28},{28,32},{32,36}... | collective-permute-start | bytes 53768 | tf_op jit(solution)/shard_map/ppermute | solution.py:29
  388.9 9.5 %collective-permute-start.17 = (f32[5,1,896]{2,1,0:T(1,128)S(1)}, f32[5,1,896]{2,1,0:T(1,128)S(1)}, u32[]{:S(2)}, u32[]{:S(2)}) collective-permute-start(f32[5,1,896]{2,1,0:T(1,128)S(1)} %get-tuple-element.18), channel_id=1, source_target_pairs={{4,0},{8,4},{12,8},{16,12},{20,16},{24,20},{28,24},{32,28},{36,32}... | collective-permute-start | bytes 53768 | tf_op jit(solution)/shard_map/ppermute | solution.py:30
  398.6 2.1 collective-permute-start.18
  398.9 4.8 %collective-permute-start.19 = (f32[5,34,1]{2,1,0:T(8,128)S(1)}, f32[5,34,1]{2,1,0:T(8,128)S(1)}, u32[]{:S(2)}, u32[]{:S(2)}) collective-permute-start(f32[5,34,1]{2,1,0:T(8,128)S(1)} %get-tuple-element.14), channel_id=1, source_target_pairs={{1,0},{2,1},{3,2},{0,3},{5,4},{6,5},{7,6},{4,7},{9,8},{10,9},{11,1... | collective-permute-start | bytes 2048 | tf_op jit(solution)/shard_map/ppermute | solution.py:30
